TPU v7x, 32 devices: a whole 2x2x4 slice. The times are simulated.
32 devices in a mesh: dp: 8 (over z, x), tensor: 4 (over y, core).
Axes of the slice: x: 2, y: 2, z: 4, core: 2. Of those that a mesh axis runs over, the one named last changes fastest.
Arguments:
- query_states: bfloat16 [1, 8192, 1024], P(None, 'dp', 'tensor'), may hold values from -6 to 6
- key_states: bfloat16 [1, 8192, 1024], P(None, 'dp', 'tensor'), may hold values from -6 to 6
- value_states: bfloat16 [1, 8192, 1024], P(None, 'dp', 'tensor'), may hold values from -6 to 6
- joining_weight: bfloat16 [1, 1024, 2048], P(None, 'tensor'), may hold values from -0.1875 to 0.1875
- norm_gain: float32 [2048], replicated, may hold values from 0.1 to 1.9
- next_hidden: bfloat16 [8192, 2048], P(('dp', 'tensor')), may hold values from -6 to 6
- lengths: int32 [8], P('dp'), may hold values from 256 to 1024
- vote_counts: int32 [8], P('dp'), may hold values from 1 to 8
Outputs:
- draft_hidden: bfloat16 [8192, 2048], P(('dp', 'tensor'))
- weight_grad: bfloat16 [1, 1024, 2048], P(None, 'tensor', 'dp')
- gain_grad: float32 [2048], replicated
- draft_loss: float32 [], replicated
All inputs are finite; a program needn't handle non-finite values.
Results may differ from a plain program's by a relative error of at most 0.014.
Values may be sent and summed in bfloat16 or wider, within the bound.
No kernel may reach another device: no remote copies, remote signals or barrier semaphores. Data moves between devices by JAX's collectives and lax.ppermute only.
A program may use at most 64 MiB of HBM per device.

v0:
```python
import math
import jax
import jax.numpy as jnp
from jax import lax
from jax.sharding import PartitionSpec as P

HD = 128
loss_scale = 65536.0
neg_large = -1e30


def on_device(
    query_states,
    key_states,
    value_states,
    joining_weight,
    norm_gain,
    next_hidden,
    lengths,
    vote_counts,
):
    n_layers, tok_group, col_width = query_states.shape
    chains = lengths.shape[0]
    seq_len = tok_group // chains
    heads_here = col_width // HD
    shaped = (n_layers, chains, seq_len, heads_here, HD)
    scores = jnp.einsum(
        "lcqhd,lckhd->lchqk",
        query_states.reshape(shaped),
        key_states.reshape(shaped),
        preferred_element_type=jnp.float32,
    ) / math.sqrt(HD)
    positions = jnp.arange(seq_len)
    causal = positions[None, :] <= positions[:, None]
    key_valid = positions[None, :] < lengths[:, None]
    visible = causal[None, None, None, :, :] & key_valid[None, :, None, None, :]
    scores = jnp.where(visible, scores, neg_large)
    row_peak = jnp.max(scores, axis=-1, keepdims=True)
    exponent = jnp.exp(scores - row_peak)
    attn_probs = (exponent / jnp.sum(exponent, axis=-1, keepdims=True)).astype(jnp.bfloat16)
    context = jnp.einsum(
        "lchqk,lckhd->lcqhd",
        attn_probs,
        value_states.reshape(shaped),
        preferred_element_type=jnp.float32,
    )
    context = context.astype(jnp.bfloat16).reshape(n_layers, tok_group, col_width)
    own_rows = next_hidden.shape[0]
    offset = lax.axis_index("tensor") * own_rows
    partial_sum = jnp.einsum(
        "ltc,lcd->td", context, joining_weight, preferred_element_type=jnp.float32
    )
    summed = lax.psum(partial_sum.astype(jnp.bfloat16), "tensor").astype(jnp.float32)
    joined_rows = lax.dynamic_slice_in_dim(summed, offset, own_rows, 0)
    token_pos = offset + jnp.arange(own_rows, dtype=jnp.int32)
    chain_of = token_pos // seq_len
    in_chain = token_pos % seq_len
    onehot = (chain_of[:, None] == jnp.arange(chains)[None, :]).astype(jnp.float32)
    tok_votes = jnp.dot(onehot, vote_counts.astype(jnp.float32), precision=lax.Precision.HIGHEST)
    tok_length = jnp.dot(onehot, lengths.astype(jnp.float32), precision=lax.Precision.HIGHEST)
    token_weight = jnp.where(in_chain.astype(jnp.float32) < tok_length - 1.0, tok_votes, 0.0)
    inv_rms = lax.rsqrt(jnp.mean(joined_rows * joined_rows, axis=-1, keepdims=True) + 1e-06)
    normed = joined_rows * inv_rms
    predicted = normed * norm_gain
    draft_hidden = predicted.astype(jnp.bfloat16)
    misfit = predicted - next_hidden.astype(jnp.float32)
    local_loss = jnp.sum(token_weight * jnp.mean(misfit * misfit, axis=-1))
    grad_pred = loss_scale * 2.0 / joined_rows.shape[1] * token_weight[:, None] * misfit
    local_gain = jnp.sum(grad_pred * normed, axis=0)
    grad_normed = grad_pred * norm_gain
    grad_joined = (
        inv_rms * (grad_normed - normed * jnp.mean(grad_normed * normed, axis=-1, keepdims=True))
    ).astype(jnp.bfloat16)
    gain_sum, loss_sum, weight_total = lax.psum(
        (local_gain, local_loss, jnp.sum(token_weight)), ("dp", "tensor")
    )
    grad_total = jnp.einsum(
        "ltc,td->lcd",
        context,
        lax.all_gather(grad_joined, "tensor", axis=0, tiled=True),
        preferred_element_type=jnp.float32,
    )
    grad_cols = lax.psum_scatter(
        grad_total.astype(jnp.bfloat16), "dp", scatter_dimension=2, tiled=True
    ).astype(jnp.float32)
    weight_grad = (grad_cols / weight_total).astype(jnp.bfloat16)
    return (draft_hidden, weight_grad, gain_sum / weight_total, loss_sum / weight_total)


def solution(mesh):
    return jax.shard_map(
        on_device,
        mesh=mesh,
        in_specs=(
            P(None, "dp", "tensor"),
            P(None, "dp", "tensor"),
            P(None, "dp", "tensor"),
            P(None, "tensor", None),
            P(),
            P(("dp", "tensor"), None),
            P("dp"),
            P("dp"),
        ),
        out_specs=(P(("dp", "tensor"), None), P(None, "tensor", "dp"), P(), P()),
        check_vma=False,
    )
```

profile of v0, /device:TPU:0, one launch (start us, length us, event | category | flops | bytes accessed | tf_op | source)
XLA Modules:
  0.0 236.3 jit_solution(4800602347688197091)
XLA Ops:
  7.2 0.0 copy-start
  7.2 0.0 copy-start.2
  7.2 0.0 copy-start.3
  7.2 0.0 all-reduce.3.cloned.1.call-start
  8.0 0.4 fusion.4
  8.4 2.0 reshape.122
  10.4 0.0 copy-done.2
  10.4 1.0 reshape.123
  11.4 0.0 copy-done.3
  11.4 1.0 copy.17
  12.4 7.7 %fusion.39 = (f32[2,1024]{1,0:T(2,128)S(1)}, f32[2,1024,1024]{1,2,0:T(8,128)}) fusion(pred[1024,1024]{0,1:T(8,128)(4,1)S(1)} %fusion.4, bf16[1024,2,128]{2,1,0:T(2,128)(2,1)} %reshape.123, bf16[1024,2,128]{2,1,0:T(2,128)(2,1)} %reshape.122), kind=kOutput, calls=%fused_computation.54 | convolution fusion | flops 545260544 | bytes 10493952 | tf_op jit(solution)/shard_map/sub | solution.py:39
  20.1 0.0 copy-done.4
  20.1 4.1 %fusion.20 = bf16[2,1024,128]{1,2,0:T(8,128)(2,1)S(1)} fusion(bf16[1024,2,128]{0,2,1:T(8,128)(2,1)S(1)} %bitcast.23, f32[2,1024,1024]{1,2,0:T(8,128)} %get-tuple-element.13, f32[2,1024]{1,0:T(2,128)S(1)} %get-tuple-element.12), kind=kOutput, calls=%fused_computation.29 | convolution fusion | flops 541327360 | bytes 9445376 | tf_op jit(solution)/shard_map/lchqk,lckhd->lcqhd/dot_general | solution.py:41
  24.3 0.0 copy-done
  24.3 3.3 %convolution_convert_fusion = bf16[1024,2048]{1,0:T(8,128)(2,1)} fusion(bf16[1024,256]{0,1:T(8,128)(2,1)S(1)} %bitcast.21, bf16[1,256,2048]{2,1,0:T(8,128)(2,1)S(1)} %copy-done), kind=kOutput, calls=%fused_computation.11 | convolution fusion | flops 1075838976 | bytes 5767168 | tf_op jit(solution)/shard_map/ltc,lcd->td/dot_general | solution.py:50
  27.5 0.0 all-reduce.3.cloned.1.call-update
  27.6 0.0 all-gather.2.cloned.1.call-start
  28.3 0.6 broadcast_multiply_fusion
  29.0 86.9 %all-reduce.3.cloned.1.call-done = bf16[1024,2048]{1,0:T(8,128)(2,1)} async-done(((bf16[1024,2048]{1,0:T(8,128)(2,1)}), bf16[1024,2048]{1,0:T(8,128)(2,1)}) %all-reduce.3.cloned.1.call-update) | async-done | bytes 4194320 | tf_op jit(solution)/shard_map/psum | solution.py:53
  115.9 1.5 fusion.19
  117.4 2.3 fusion.18
  119.8 3.4 %fusion.17 = (bf16[256,2048]{1,0:T(8,128)(2,1)}, bf16[256,2048]{1,0:T(8,128)(2,1)}) fusion(bf16[256,2048]{1,0:T(8,128)(2,1)S(1)} %copy-done.1, f32[256]{0:T(256)S(1)} %broadcast_multiply_fusion.1, f32[256]{0:T(256)S(1)} %get-tuple-element.14, f32[2048]{0:T(1024)S(1)} %copy-done.5, f32[256]{0:T(256)S(1)} %add_rsqrt_fusion, ...), kind=kLoop, calls=%fused_computation.25 | loop fusion | flops 6291456 | bytes 4205572 | tf_op jit(solution)/shard_map/convert_element_type | solution.py:73
  123.2 0.0 all-gather.2.cloned.1.call-update
  123.2 0.0 reduce-scatter.2.cloned.1.call-start
  123.3 34.7 %all-gather.2.cloned.1.call-done = bf16[1024,2048]{1,0:T(8,128)(2,1)} async-done(((bf16[256,2048]{1,0:T(8,128)(2,1)}), bf16[1024,2048]{1,0:T(8,128)(2,1)}) %all-gather.2.cloned.1.call-update) | async-done | bytes 4194320 | tf_op jit(solution)/shard_map/all_gather | solution.py:80
  158.0 4.4 %fusion.11 = bf16[1,256,2048]{2,1,0:T(8,128)(2,1)} fusion(bf16[1024,256]{0,1:T(8,128)(2,1)S(1)} %bitcast.22, bf16[1024,2048]{1,0:T(8,128)(2,1)} %all-gather.2.cloned.1.call-done), kind=kOutput, calls=%fused_computation.19 | convolution fusion | flops 1074266112 | bytes 5767168 | tf_op jit(solution)/shard_map/ltc,td->lcd/dot_general | solution.py:77
  162.4 0.0 reduce-scatter.2.cloned.1.call-update
  162.4 0.7 multiply_reduce_fusion.1
  163.1 39.7 %all-reduce = (f32[]{:T(128)}, f32[2048]{0:T(1024)S(1)}, f32[]{:T(128)}) all-reduce(f32[]{:T(128)} %get-tuple-element.15, f32[2048]{0:T(1024)S(1)} %get-tuple-element.4, f32[]{:T(128)} %multiply_reduce_fusion.1), channel_id=1, replica_groups=mesh['dp'=8,'tensor'=4] {'dp','tensor'}, use_global_device_ids=true, to_apply=%region_7.8 | all-reduce | flops 2050 | bytes 16400 | tf_op jit(solution)/shard_map/psum | solution.py:74
  204.1 1.2 broadcast_divide_fusion
  205.2 21.3 %reduce-scatter.2.cloned.1.call-done = bf16[1,256,256]{2,1,0:T(8,128)(2,1)} async-done(((bf16[1,256,2048]{2,1,0:T(8,128)(2,1)}), bf16[1,256,256]{2,1,0:T(8,128)(2,1)}) %reduce-scatter.2.cloned.1.call-update) | async-done | bytes 131088 | tf_op jit(solution)/shard_map/reduce_scatter | solution.py:83
  226.5 2.1 divide_convert_fusion.4
  (8 shorter events, 0.0 us)
Async XLA Ops:
  7.2 17.1 %copy-start = (bf16[1,256,2048]{2,1,0:T(8,128)(2,1)S(1)}, bf16[1,256,2048]{2,1,0:T(8,128)(2,1)}, u32[]{:S(2)}) copy-start(bf16[1,256,2048]{2,1,0:T(8,128)(2,1)} %param.11) | copy-start | bytes 3145732
  7.2 3.3 %copy-start.2 = (bf16[1,1024,256]{2,1,0:T(8,128)(2,1)S(1)}, bf16[1,1024,256]{2,1,0:T(8,128)(2,1)}, u32[]{:S(2)}) copy-start(bf16[1,1024,256]{2,1,0:T(8,128)(2,1)} %param.9) | copy-start | bytes 1572868
  7.2 4.2 %copy-start.3 = (bf16[1,1024,256]{2,1,0:T(8,128)(2,1)S(1)}, bf16[1,1024,256]{2,1,0:T(8,128)(2,1)}, u32[]{:S(2)}) copy-start(bf16[1,1024,256]{2,1,0:T(8,128)(2,1)} %param.10) | copy-start | bytes 1572868
  7.2 108.7 %all-reduce.3.cloned.1.call-start = ((), (), s32[]{:S(2)}) async-start(), calls=%async_computation.1 | async-start | bytes 8388608 | tf_op jit(solution)/shard_map/psum | solution.py:53
  12.4 7.7 %copy-start.4 = (bf16[1,1024,256]{1,2,0:T(8,128)(2,1)S(1)}, bf16[1,1024,256]{1,2,0:T(8,128)(2,1)}, u32[]{:S(2)}) copy-start(bf16[1,1024,256]{1,2,0:T(8,128)(2,1)} %copy.17) | copy-start | bytes 1572868
  27.5 89.9 %copy-start.1 = (bf16[256,2048]{1,0:T(8,128)(2,1)S(1)}, bf16[256,2048]{1,0:T(8,128)(2,1)}, u32[]{:S(2)}) copy-start(bf16[256,2048]{1,0:T(8,128)(2,1)} %param.13) | copy-start | bytes 3145732
  27.5 89.9 %copy-start.5 = (f32[2048]{0:T(1024)S(1)}, f32[2048]{0:T(1024)}, u32[]{:S(2)}) copy-start(f32[2048]{0:T(1024)} %param.12) | copy-start | bytes 24580
  27.6 130.4 %all-gather.2.cloned.1.call-start = ((), (), s32[]{:S(2)}) async-start(), calls=%async_computation.2 | async-start | bytes 5242880 | tf_op jit(solution)/shard_map/all_gather | solution.py:80
  123.2 103.3 %reduce-scatter.2.cloned.1.call-start = ((), (), s32[]{:S(2)}) async-start(), calls=%async_computation.3 | async-start | bytes 1179648 | tf_op jit(solution)/shard_map/reduce_scatter | solution.py:83
Sparse Core Ops, SparseCore 0:
  27.7 88.1 all-reduce.2
  123.3 34.6 all-gather.1
  162.5 63.9 reduce-scatter.1
where the time goes:
time: 237 us; the launch traced here: 236 us
  waiting for transfers between devices  143 us (60%)
  blocking collectives  39.7 us (17%)
  matrix products  19.5 us (8%)
  between operations  17.7 us (7%)
  other arithmetic  12.2 us (5%)
  local copies, waits for them, and re-layouts  4.04 us (2%)
    psum x1, waiting for transfers between devices, on_device(): lax.psum(partial_sum.astype(jnp.bfloat16), 'tensor').astype(jnp.float32)  86.9 us
    psum x1, blocking collectives, on_device(): lax.psum((local_gain, local_loss, jnp.sum(token_weight)), ('dp', 'tensor'))  39.7 us
    all_gather x1, waiting for transfers between devices, on_device(): lax.all_gather(grad_joined, 'tensor', axis=0, tiled=True)  34.7 us
    reduce_scatter x1, waiting for transfers between devices, on_device(): lax.psum_scatter(grad_total.astype(jnp.bfloat16), 'dp', scatter_dimension...  21.3 us
    sub x1, matrix products, on_device(): exponent = jnp.exp(scores - row_peak)  7.73 us
  transfers between devices with their start and end apart: 3, of which 3 were waited for; matrix products, arithmetic and copies ran while one was open for 1% of the time, Pallas kernels for 0%

commit v1 on v0

--- a/solution.py
+++ b/solution.py
@@ -7,6 +7,18 @@
 HD = 128
 loss_scale = 65536.0
 neg_large = -1e30
+
+
+def gather_by_bits(x, axis, dim):
+    ways, here = (lax.axis_size(axis), lax.axis_index(axis))
+    grown, reach = (x, 1)
+    while reach < ways:
+        theirs = lax.ppermute(grown, axis, [(d, d ^ reach) for d in range(ways)])
+        mine_first = jnp.concatenate([grown, theirs], axis=dim)
+        theirs_first = jnp.concatenate([theirs, grown], axis=dim)
+        grown = jnp.where(here & reach == 0, mine_first, theirs_first)
+        reach = 2 * reach
+    return grown
 
 
 def on_device(
@@ -77,7 +89,7 @@
     grad_total = jnp.einsum(
         "ltc,td->lcd",
         context,
-        lax.all_gather(grad_joined, "tensor", axis=0, tiled=True),
+        gather_by_bits(grad_joined, "tensor", 0),
         preferred_element_type=jnp.float32,
     )
     grad_cols = lax.psum_scatter(

time: 237 us -> 259 us (1.093)
  waiting for transfers between devices: 143 us -> 159 us
  other arithmetic: 12.2 us -> 15.7 us
    ppermute x0 -> x2, waiting for transfers between devices: none -> 50.3 us  [gather_by_bits(): theirs = lax.ppermute(grown, axis, [(d, d ^ reach) for d in range(ways)])]
    all_gather x1 -> x0, waiting for transfers between devices: 34.7 us -> none  [on_device(): lax.all_gather(grad_joined, 'tensor', axis=0, tiled=True)]
    select_n x0 -> x1, other arithmetic: none -> 3.82 us  [gather_by_bits(): grown = jnp.where(here & reach == 0, mine_first, theirs_first)]
  transfers between devices with their start and end apart: 3 -> 4, of which waited for: 3 -> 4; matrix products, arithmetic and copies ran while one was open for 1% -> 1% of each run, Pallas kernels for 0% -> 0%
where the time goes in v1:
time: 259 us
  waiting for transfers between devices  159 us (61%)
  blocking collectives  39.9 us (15%)
  matrix products  20.7 us (8%)
  between operations  18 us (7%)
  other arithmetic  15.7 us (6%)
  local copies, waits for them, and re-layouts  5.23 us (2%)
    psum x1, waiting for transfers between devices, on_device(): lax.psum(partial_sum.astype(jnp.bfloat16), 'tensor').astype(jnp.float32)  87.5 us
    ppermute x2, waiting for transfers between devices, gather_by_bits(): theirs = lax.ppermute(grown, axis, [(d, d ^ reach) for d in range(ways)])  50.3 us
    psum x1, blocking collectives, on_device(): lax.psum((local_gain, local_loss, jnp.sum(token_weight)), ('dp', 'tensor'))  39.9 us
    reduce_scatter x1, waiting for transfers between devices, on_device(): lax.psum_scatter(grad_total.astype(jnp.bfloat16), 'dp', scatter_dimension...  20.7 us
    sub x1, matrix products, on_device(): exponent = jnp.exp(scores - row_peak)  7.53 us
    dot_general x1, matrix products, on_device(): jnp.einsum('ltc,td->lcd', context, gather_by_bits(grad_joined, 'tensor',...  5.74 us
  transfers between devices with their start and end apart: 4, of which 4 were waited for; matrix products, arithmetic and copies ran while one was open for 1% of the time, Pallas kernels for 0%

profile of v1, /device:TPU:0, one launch (start us, length us, event | category | flops | bytes accessed | tf_op | source)
XLA Modules:
  0.0 258.6 jit_solution(17393535471957651559)
XLA Ops:
  7.2 0.0 copy-start
  7.2 0.0 all-reduce.3.cloned.1.call-start
  8.0 0.4 fusion.10
  8.3 1.2 reshape.122
  9.5 2.0 reshape.123
  11.5 1.2 copy.17
  12.7 7.5 %fusion.48 = (f32[2,1024]{1,0:T(2,128)S(1)}, f32[2,1024,1024]{1,2,0:T(8,128)}) fusion(pred[1024,1024]{0,1:T(8,128)(4,1)S(1)} %fusion.10, bf16[1024,2,128]{2,1,0:T(2,128)(2,1)} %reshape.123, bf16[1024,2,128]{2,1,0:T(2,128)(2,1)S(1)} %reshape.122), kind=kOutput, calls=%fused_computation.64 | convolution fusion | flops 545260544 | bytes 10493952 | tf_op jit(solution)/shard_map/sub | solution.py:51
  20.2 4.1 %fusion.28 = bf16[2,1024,128]{1,2,0:T(8,128)(2,1)S(1)} fusion(bf16[1024,2,128]{0,2,1:T(8,128)(2,1)S(1)} %bitcast.22, f32[2,1024,1024]{1,2,0:T(8,128)} %get-tuple-element.13, f32[2,1024]{1,0:T(2,128)S(1)} %get-tuple-element.12), kind=kOutput, calls=%fused_computation.38 | convolution fusion | flops 541327360 | bytes 9445376 | tf_op jit(solution)/shard_map/lchqk,lckhd->lcqhd/dot_general | solution.py:53
  24.4 0.0 copy-start.2
  24.4 0.8 copy-done.2
  25.2 0.0 copy-done
  25.2 3.3 %convolution_convert_fusion = bf16[1024,2048]{1,0:T(8,128)(2,1)} fusion(bf16[1024,256]{0,1:T(8,128)(2,1)S(1)} %bitcast.20, bf16[1,256,2048]{2,1,0:T(8,128)(2,1)S(1)} %copy-done), kind=kOutput, calls=%fused_computation.19 | convolution fusion | flops 1075838976 | bytes 5767168 | tf_op jit(solution)/shard_map/ltc,lcd->td/dot_general | solution.py:62
  28.5 0.0 all-reduce.3.cloned.1.call-update
  28.5 0.0 reduce-scatter.2.cloned.1.call-start
  29.3 87.5 %all-reduce.3.cloned.1.call-done = bf16[1024,2048]{1,0:T(8,128)(2,1)} async-done(((bf16[1024,2048]{1,0:T(8,128)(2,1)}), bf16[1024,2048]{1,0:T(8,128)(2,1)}) %all-reduce.3.cloned.1.call-update) | async-done | bytes 4194320 | tf_op jit(solution)/shard_map/psum | solution.py:65
  116.9 1.5 fusion.27
  118.4 2.3 fusion.26
  120.8 3.0 %fusion.25 = (bf16[256,2048]{1,0:T(8,128)(2,1)S(1)}, bf16[256,2048]{1,0:T(8,128)(2,1)}) fusion(bf16[256,2048]{1,0:T(8,128)(2,1)S(1)} %copy-done.1, f32[256]{0:T(256)S(1)} %broadcast_multiply_fusion.1, f32[256]{0:T(256)S(1)} %broadcast_multiply_fusion, f32[2048]{0:T(1024)S(1)} %copy-done.4, f32[256]{0:T(256)S(1)} %add_rsqrt_fusion, ...), kind=kLoop, calls=%fused_computation.33 | loop fusion | flops 6291456 | bytes 4205572 | tf_op jit(solution)/shard_map/convert_element_type | solution.py:85
  123.8 0.0 collective-permute-start
  123.8 2.8 %collective-permute-done = bf16[256,2048]{1,0:T(8,128)(2,1)} collective-permute-done((bf16[256,2048]{1,0:T(8,128)(2,1)S(1)}, bf16[256,2048]{1,0:T(8,128)(2,1)}, u32[]{:S(2)}, u32[]{:S(2)}) %collective-permute-start) | collective-permute-done | bytes 1048608 | tf_op jit(solution)/shard_map/ppermute | solution.py:16
  126.6 3.8 %maximum_select_fusion.6 = bf16[512,2048]{1,0:T(8,128)(2,1)} fusion(bf16[256,2048]{1,0:T(8,128)(2,1)} %collective-permute-done, bf16[256,2048]{1,0:T(8,128)(2,1)S(1)} %get-tuple-element.10, pred[]{:T(512)S(6)} %eq.17), kind=kLoop, calls=%fused_computation.36 | loop fusion | flops 9437184 | bytes 4194305 | tf_op jit(solution)/shard_map/jit(_where)/select_n | solution.py:19
  130.4 0.5 collective-permute-start.1
  130.9 47.5 %collective-permute-done.1 = bf16[512,2048]{1,0:T(8,128)(2,1)} collective-permute-done((bf16[512,2048]{1,0:T(8,128)(2,1)}, bf16[512,2048]{1,0:T(8,128)(2,1)}, u32[]{:S(2)}, u32[]{:S(2)}) %collective-permute-start.1) | collective-permute-done | bytes 2097184 | tf_op jit(solution)/shard_map/ppermute | solution.py:16
  178.4 0.0 copy-done.3
  178.4 5.7 %fusion.19 = bf16[1,256,2048]{2,1,0:T(8,128)(2,1)} fusion(bf16[1024,256]{0,1:T(8,128)(2,1)S(1)} %bitcast.21, bf16[512,2048]{1,0:T(8,128)(2,1)} %collective-permute-done.1, bf16[512,2048]{1,0:T(8,128)(2,1)} %maximum_select_fusion.6, pred[]{:T(512)S(6)} %eq.16), kind=kOutput, calls=%fused_computation.27 | convolution fusion | flops 1093140480 | bytes 5767169 | tf_op jit(solution)/shard_map/ltc,td->lcd/dot_general | solution.py:89
  184.1 0.0 reduce-scatter.2.cloned.1.call-update
  184.2 0.6 fusion.44
  184.8 0.7 multiply_reduce_fusion.1
  185.4 39.9 %all-reduce = (f32[]{:T(128)}, f32[2048]{0:T(1024)S(1)}, f32[]{:T(128)}) all-reduce(f32[]{:T(128)} %fusion.44, f32[2048]{0:T(1024)S(1)} %get-tuple-element.4, f32[]{:T(128)} %multiply_reduce_fusion.1), channel_id=1, replica_groups=mesh['dp'=8,'tensor'=4] {'dp','tensor'}, use_global_device_ids=true, to_apply=%region_7.8 | all-reduce | flops 2050 | bytes 16400 | tf_op jit(solution)/shard_map/psum | solution.py:86
  226.6 1.2 broadcast_divide_fusion
  227.7 20.7 %reduce-scatter.2.cloned.1.call-done = bf16[1,256,256]{2,1,0:T(8,128)(2,1)} async-done(((bf16[1,256,2048]{2,1,0:T(8,128)(2,1)}), bf16[1,256,256]{2,1,0:T(8,128)(2,1)}) %reduce-scatter.2.cloned.1.call-update) | async-done | bytes 131088 | tf_op jit(solution)/shard_map/reduce_scatter | solution.py:95
  248.5 2.1 divide_convert_fusion.4
  (9 shorter events, 0.0 us)
Async XLA Ops:
  7.2 18.0 %copy-start = (bf16[1,256,2048]{2,1,0:T(8,128)(2,1)S(1)}, bf16[1,256,2048]{2,1,0:T(8,128)(2,1)}, u32[]{:S(2)}) copy-start(bf16[1,256,2048]{2,1,0:T(8,128)(2,1)} %param.11) | copy-start | bytes 3145732
  7.2 109.7 %all-reduce.3.cloned.1.call-start = ((), (), s32[]{:S(2)}) async-start(), calls=%async_computation.1 | async-start | bytes 8388608 | tf_op jit(solution)/shard_map/psum | solution.py:65
  24.4 0.8 copy-start.2
  28.5 89.9 %copy-start.1 = (bf16[256,2048]{1,0:T(8,128)(2,1)S(1)}, bf16[256,2048]{1,0:T(8,128)(2,1)}, u32[]{:S(2)}) copy-start(bf16[256,2048]{1,0:T(8,128)(2,1)} %param.13) | copy-start | bytes 3145732
  28.5 89.9 %copy-start.4 = (f32[2048]{0:T(1024)S(1)}, f32[2048]{0:T(1024)}, u32[]{:S(2)}) copy-start(f32[2048]{0:T(1024)} %param.12) | copy-start | bytes 24580
  28.5 220.0 %reduce-scatter.2.cloned.1.call-start = ((), (), s32[]{:S(2)}) async-start(), calls=%async_computation.2 | async-start | bytes 1179648 | tf_op jit(solution)/shard_map/reduce_scatter | solution.py:95
  123.8 54.6 %copy-start.3 = (bf16[2,1024,128]{1,2,0:T(8,128)(2,1)S(1)}, bf16[2,1024,128]{1,2,0:T(8,128)(2,1)}, u32[]{:S(2)}) copy-start(bf16[2,1024,128]{1,2,0:T(8,128)(2,1)} %copy-done.2) | copy-start | bytes 1572868
  123.8 2.8 %collective-permute-start = (bf16[256,2048]{1,0:T(8,128)(2,1)S(1)}, bf16[256,2048]{1,0:T(8,128)(2,1)}, u32[]{:S(2)}, u32[]{:S(2)}) collective-permute-start(bf16[256,2048]{1,0:T(8,128)(2,1)S(1)} %get-tuple-element.10), channel_id=1, source_target_pairs={{0,1},{1,0},{2,3},{3,2},{4,5},{5,4},{6,7},{7,6},{8,9},{9,8},{10,11... | collective-permute-start | bytes 3145736 | tf_op jit(solution)/shard_map/ppermute | solution.py:16
  130.4 48.0 %collective-permute-start.1 = (bf16[512,2048]{1,0:T(8,128)(2,1)}, bf16[512,2048]{1,0:T(8,128)(2,1)}, u32[]{:S(2)}, u32[]{:S(2)}) collective-permute-start(bf16[512,2048]{1,0:T(8,128)(2,1)} %maximum_select_fusion.6), channel_id=1, source_target_pairs={{0,2},{1,3},{2,0},{3,1},{4,6},{5,7},{6,4},{7,5},{8,10},{9,11},{10,... | collective-permute-start | bytes 6291464 | tf_op jit(solution)/shard_map/ppermute | solution.py:16
Sparse Core Ops, SparseCore 0:
  28.6 88.1 all-reduce.2
  184.3 64.1 reduce-scatter.1
